TPU v7x, 128 devices: a whole 4x4x4 slice. The times are simulated.
128 devices in a mesh: angle: 8 (over x_hi, y), row: 16 (over z, x_lo, core).
Axes of the slice: x: 4 (x_hi: 2, x_lo: 2; x = x_hi * 2 + x_lo), y: 4, z: 4, core: 2. Of those that a mesh axis runs over, the one named last changes fastest.
Arguments:
- intensity: float32 [1024, 16, 4096], P('angle', 'row'), may hold values from 0.036 to 1
- flat_field: float32 [16, 4096], P('row'), may hold values from 1 to 2
- dark_field: float32 [16, 4096], P('row'), may hold values from 0 to 0.02
- correlation: int32 [1], replicated, may hold values from 512 to 1536
- blend_width: int32 [1], replicated, may hold values from 64 to 511
- padding: int32 [1], replicated, may hold values from 1024 to 4096
- cutoff: int32 [1], replicated, may hold values from 1 to 8
Outputs:
- sinogram: float32 [512, 16, 8192], P('angle', 'row')
All inputs are finite; a program needn't handle non-finite values.
Results may differ from a plain program's by a relative error of at most 0.00023.
Values sent between devices are 32-bit elements; how exact they have to be, the bound alone decides.
A program may use at most 128 MiB of HBM per device.

v0:
```python
import functools
import math

import jax
import jax.numpy as jnp
import numpy as np
from jax import lax
from jax.experimental import pallas as pl
from jax.experimental.pallas import tpu as pltpu
from jax.sharding import PartitionSpec as P

KMAX = 8
FCUT = 512
LANE = 128
MODES = 16
CHUNK = 8
STACK = 80


def split_np(table):
    high = table.astype(jnp.bfloat16)
    low = (table - high.astype(np.float64)).astype(jnp.bfloat16)
    return high, low


def split(value):
    high = value.astype(jnp.bfloat16)
    low = (value - high.astype(jnp.float32)).astype(jnp.bfloat16)
    return high, low


def split_outside(value):
    high = lax.reduce_precision(value, 8, 7)
    return high.astype(jnp.bfloat16), (value - high).astype(jnp.bfloat16)


@functools.cache
def constants(length):
    kept = length // 2
    freq = np.arange(kept, dtype=np.float64)
    ramp = freq / kept * (1.0 + np.cos(np.pi * freq / kept))
    drop = 1.0 - 1.0 / (1.0 + (freq / FCUT) ** 8)
    half = LANE // 2
    gains, sums = [], []
    reach = length * 3 // 4
    for gain in (ramp, ramp * drop):
        full = np.zeros(length)
        full[:kept] = gain
        full[kept + 1 :] = gain[:0:-1]
        kernel = np.fft.ifft(full).real
        offsets = np.arange(-reach, reach + 1)
        sums.append(np.concatenate([[0.0], np.cumsum(kernel[offsets % length])]))
        place = np.arange(length)
        signed = np.where(place < kept, place, place - length)
        turned = kernel * np.exp(-1j * np.pi * signed / length)
        turned[kept] = 0.0
        between = np.fft.fft(turned).real
        k1 = np.arange(half)[:, None]
        k2 = np.arange(LANE)[None, :]
        gains.append(between[k1 + LANE * k2] * (2.0 / length))
    k1 = np.arange(half)[:, None]
    n2 = np.arange(LANE)[None, :]
    turn = 2.0 * np.pi * (k1 + 0.5) * n2 / length
    twiddle = np.stack([np.cos(turn), np.sin(turn)]).astype(np.float32)
    a = np.arange(LANE)[:, None]
    b = np.arange(LANE)[None, :]
    angle = 2.0 * np.pi * (a * b % LANE) / LANE
    c, s = np.cos(angle), np.sin(angle)
    forward = split_np(np.block([[c, -s], [s, c]]))
    backward = split_np(np.block([[c, s], [-s, c]]))
    n1 = np.arange(half)[:, None]
    last = 2.0 * np.pi * ((2 * np.arange(half)[None, :] + 1) * n1 % (2 * LANE)) / (2 * LANE)
    high, low = split_np(np.concatenate([np.cos(last), -np.sin(last)], axis=1))
    final = np.concatenate([high, high, low], axis=1)
    return (
        np.stack(gains).astype(np.float32),
        np.stack(sums).astype(np.float32),
        twiddle,
        np.concatenate([forward[0], forward[1]], axis=0),
        np.concatenate([backward[0], backward[1]], axis=0),
        final,
        reach,
    )


def dot(a, b):
    return jnp.dot(a, b, preferred_element_type=jnp.float32)


def modes_kernel(x_ref, flat_ref, dark_ref, phi_ref, o_ref):
    count = phi_ref.shape[1] // 3
    blocks = flat_ref.shape[0]
    phi = phi_ref[...]
    for n1 in range(blocks):
        dark = dark_ref[n1 : n1 + 1, :]
        base = jnp.log(flat_ref[n1 : n1 + 1, :] - dark)
        rows = x_ref[pl.ds(n1, count, stride=blocks), :]
        high, low = split(base - jnp.log(rows - dark))
        o_ref[pl.ds(n1, MODES, stride=blocks), :] = dot(phi, jnp.concatenate([high, low, high], axis=0))


def modes(x, flat, dark, phi):
    blocks = flat.shape[0]
    return pl.pallas_call(
        modes_kernel,
        out_shape=jax.ShapeDtypeStruct((MODES * blocks, LANE), jnp.float32),
        in_specs=[pl.BlockSpec(memory_space=pltpu.VMEM)] * 4,
        out_specs=pl.BlockSpec(memory_space=pltpu.VMEM),
        compiler_params=pltpu.CompilerParams(vmem_limit_bytes=32 << 20),
        cost_estimate=pl.CostEstimate(flops=50000000, bytes_accessed=3000000, transcendentals=600000),
        name="modes",
    )(x, flat, dark, phi)


def main_kernel(
    s_ref,
    own_ref,
    got_ref,
    gm_ref,
    gb_ref,
    flat_ref,
    dark_ref,
    first_ref,
    coef_ref,
    edge_ref,
    gain_ref,
    tw_ref,
    fwd_ref,
    bwd_ref,
    fin_ref,
    out_ref,
    main_s,
    back_s,
    shift_s,
    yh_s,
    yl_s,
    res_s,
    bg_s,
    corr_s,
    edge_s,
):
    step = pl.program_id(0)
    mode_steps = MODES // CHUNK
    half = LANE // 2
    upper = s_ref[0]
    roll_by = s_ref[1]
    halfcorr = s_ref[2].astype(jnp.float32) * 0.5
    blend = s_ref[3].astype(jnp.float32)
    blocks = flat_ref.shape[0]

    is_mode = step < mode_steps

    @pl.when(is_mode)
    def _():
        main_s[...] = gm_ref[...]
        back_s[...] = gb_ref[...]

    @pl.when(jnp.logical_not(is_mode))
    def _():
        dark = dark_ref[...]
        base = jnp.log(flat_ref[...] - dark)
        own = base - jnp.log(own_ref[...] - dark)
        got = base - jnp.log(got_ref[...] - dark)
        main_s[...] = jnp.where(upper == 1, got, own)
        back_s[...] = jnp.where(upper == 1, own, got)

    @pl.when(step == 0)
    def _():
        shift_s[...] = jnp.zeros_like(shift_s)

    pixel = (
        lax.broadcasted_iota(jnp.int32, (blocks, LANE), 0) * LANE
        + lax.broadcasted_iota(jnp.int32, (blocks, LANE), 1)
    ).astype(jnp.float32)
    weight = jnp.clip((pixel + 0.5 - halfcorr) / blend + 0.5, 0.0, 1.0)
    lanes = lax.broadcasted_iota(jnp.int32, (blocks, LANE), 1)
    lanes48 = lax.broadcasted_iota(jnp.int32, (STACK - blocks, LANE), 1)
    tall = shift_s.shape[1]
    for t in range(0, CHUNK, 2):
        parts = []
        for i in (t, t + 1):
            main = main_s[i]
            back = back_s[i]
            edge_s[0, i : i + 1, :] = jnp.broadcast_to(main[blocks - 1 : blocks, LANE - 1 :], (1, LANE))
            edge_s[1, i : i + 1, :] = jnp.broadcast_to(back[blocks - 1 : blocks, LANE - 1 :], (1, LANE))
            left = jnp.take_along_axis(back * weight, LANE - 1 - lanes, axis=1)
            shift_s[i, 8 : 8 + blocks, :] = pltpu.roll(main * weight, roll_by, 1)
            here = shift_s[i, 8 : 8 + STACK - blocks, :]
            prev = shift_s[i, 7 : 7 + STACK - blocks, :]
            right = jnp.where(lanes48 >= roll_by, here, prev)
            parts.append(jnp.concatenate([left, right], axis=0))
        high, low = split(jnp.concatenate(parts, axis=1))
        y = dot(first_ref[...], jnp.concatenate([high, low, high], axis=0))
        cos, sin = tw_ref[0], tw_ref[1]
        for j, i in enumerate((t, t + 1)):
            re = y[:half, j * LANE : (j + 1) * LANE]
            im = y[half:, j * LANE : (j + 1) * LANE]
            turned = jnp.concatenate([re * cos + im * sin, im * cos - re * sin], axis=1)
            high, low = split(turned)
            yh_s[i * half : (i + 1) * half, :] = high
            yl_s[i * half : (i + 1) * half, :] = low
    wide = 2 * LANE
    which = is_mode.astype(jnp.int32)
    gain = gain_ref[which]
    gain2 = jnp.concatenate([gain, gain], axis=1)
    for t in range(0, CHUNK, 2):
        rows = slice(t * half, (t + 2) * half)
        z = (
            dot(yh_s[rows, :], fwd_ref[:wide, :])
            + dot(yl_s[rows, :], fwd_ref[:wide, :])
            + dot(yh_s[rows, :], fwd_ref[wide:, :])
        )
        z = z * jnp.concatenate([gain2, gain2], axis=0)
        high, low = split(z)
        u = dot(high, bwd_ref[:wide, :]) + dot(low, bwd_ref[:wide, :]) + dot(high, bwd_ref[wide:, :])
        parts = []
        cos, sin = tw_ref[0], tw_ref[1]
        for j in range(2):
            re = u[j * half : (j + 1) * half, :LANE]
            im = u[j * half : (j + 1) * half, LANE:]
            parts.append(jnp.concatenate([re * cos - im * sin, im * cos + re * sin], axis=0))
        high, low = split(jnp.concatenate(parts, axis=1))
        o = dot(fin_ref[...], jnp.concatenate([high, low, high], axis=0))
        for j in range(2):
            i = t + j
            res_s[i] = (
                o[:, j * LANE : (j + 1) * LANE]
                + edge_s[0, i : i + 1, :] * edge_ref[which, 0]
                + edge_s[1, i : i + 1, :] * edge_ref[which, 1]
            )

    @pl.when(is_mode)
    def _():
        for i in range(CHUNK):
            bg_s[pl.ds((step * CHUNK + i) * half, half), :] = res_s[i]

    @pl.when(step == mode_steps - 1)
    def _():
        count = coef_ref.shape[0]
        for n1 in range(half):
            high, low = split(bg_s[pl.ds(n1, MODES, stride=half), :])
            corr_s[pl.ds(n1, count, stride=half), :] = dot(
                coef_ref[...], jnp.concatenate([high, low, high], axis=0)
            )

    @pl.when(jnp.logical_not(is_mode))
    def _():
        for i in range(CHUNK):
            row = ((step - mode_steps) * CHUNK + i) * half
            out_ref[i] = res_s[i] + corr_s[pl.ds(row, half), :]


def filter_rows(scalars, own, got, gm, gb, flat, dark, first, coef, edge, gain, tw, fwd, bwd, fin):
    count = got.shape[0]
    blocks = flat.shape[0]
    half = LANE // 2
    mode_steps = MODES // CHUNK
    halves = count // CHUNK

    def whole(a):
        return pl.BlockSpec(a.shape, lambda i, s, n=a.ndim: (0,) * n)

    def rows(i, s):
        return (jnp.maximum(i - mode_steps, 0), 0, 0)

    grid_spec = pltpu.PrefetchScalarGridSpec(
        num_scalar_prefetch=1,
        grid=(mode_steps + halves,),
        in_specs=[
            pl.BlockSpec(
                (CHUNK, blocks, LANE), lambda i, s: (s[0] * halves + jnp.maximum(i - mode_steps, 0), 0, 0)
            ),
            pl.BlockSpec((CHUNK, blocks, LANE), rows),
            pl.BlockSpec((CHUNK, blocks, LANE), lambda i, s: (jnp.minimum(i, mode_steps - 1), 0, 0)),
            pl.BlockSpec((CHUNK, blocks, LANE), lambda i, s: (jnp.minimum(i, mode_steps - 1), 0, 0)),
            *[whole(a) for a in (flat, dark, first, coef, edge, gain, tw, fwd, bwd, fin)],
        ],
        out_specs=pl.BlockSpec((CHUNK, half, LANE), rows),
        scratch_shapes=[
            pltpu.VMEM((CHUNK, blocks, LANE), jnp.float32),
            pltpu.VMEM((CHUNK, blocks, LANE), jnp.float32),
            pltpu.VMEM((CHUNK, STACK - blocks + 8, LANE), jnp.float32),
            pltpu.VMEM((CHUNK * half, 2 * LANE), jnp.bfloat16),
            pltpu.VMEM((CHUNK * half, 2 * LANE), jnp.bfloat16),
            pltpu.VMEM((CHUNK, half, LANE), jnp.float32),
            pltpu.VMEM((MODES * half, LANE), jnp.float32),
            pltpu.VMEM((count * half, LANE), jnp.float32),
            pltpu.VMEM((2, CHUNK, LANE), jnp.float32),
        ],
    )
    return pl.pallas_call(
        main_kernel,
        out_shape=jax.ShapeDtypeStruct((count, half, LANE), jnp.float32),
        grid_spec=grid_spec,
        compiler_params=pltpu.CompilerParams(vmem_limit_bytes=40 << 20),
        cost_estimate=pl.CostEstimate(flops=10000000000, bytes_accessed=6000000, transcendentals=600000),
        name="filter_rows",
    )(scalars, own, got, gm, gb, flat, dark, first, coef, edge, gain, tw, fwd, bwd, fin)


def phase(orders, angles, half_turn):
    turn = (orders[:, None] * angles[None, :] % half_turn).astype(jnp.float32) * (2.0 * math.pi / half_turn)
    return jnp.concatenate([jnp.cos(turn), jnp.sin(turn)], axis=0)


def local(intensity, flat_field, dark_field, correlation, blend_width, padding, cutoff):
    angle_count = lax.axis_size("angle")
    place = lax.axis_index("angle")
    total = intensity.shape[0]
    half_block = total // 2
    pixels = intensity.shape[2]
    length = 4 * pixels
    blocks = pixels // LANE
    half = LANE // 2
    halves = angle_count // 2
    half_turn = half_block * angle_count
    upper = (place >= halves).astype(jnp.int32)
    gains, sums, tw, fwd, bwd, fin, reach = constants(length)

    x = intensity.reshape(total, blocks, LANE)
    flat = flat_field.reshape(blocks, LANE)
    dark = dark_field.reshape(blocks, LANE)
    outgoing = lax.dynamic_slice_in_dim(x, (1 - upper) * half_block, half_block, 0)
    pairs = [(source, source ^ halves) for source in range(angle_count)]
    got = lax.ppermute(outgoing, "angle", pairs)

    orders = jnp.arange(KMAX, dtype=jnp.int32)
    own_angles = place % halves * total + jnp.arange(total, dtype=jnp.int32)
    phi_high, phi_low = split_outside(phase(orders, own_angles, half_turn))
    mine = modes(
        x.reshape(total * blocks, LANE), flat, dark, jnp.concatenate([phi_high, phi_high, phi_low], axis=1)
    )
    slots = jnp.where(jnp.arange(2)[:, None, None] == upper, mine[None], 0.0)
    both = lax.psum(slots, "angle").reshape(2, MODES, blocks, LANE)

    shift = pixels - correlation[0]
    q, r = shift // LANE, shift % LANE
    k1 = jnp.arange(half, dtype=jnp.int32)[:, None]
    index = jnp.concatenate(
        [blocks - 1 - jnp.arange(blocks, dtype=jnp.int32), q + jnp.arange(STACK - blocks, dtype=jnp.int32)]
    )[None, :]
    turn = ((2 * k1 + 1) * index % (2 * LANE)).astype(jnp.float32) * (math.pi / LANE)
    high, low = split_outside(jnp.concatenate([jnp.cos(turn), -jnp.sin(turn)], axis=0))
    first = jnp.concatenate([high, high, low], axis=1)

    out_angles = place % halves * total + upper * half_block + jnp.arange(half_block, dtype=jnp.int32)
    scale = jnp.where(orders < cutoff[0], jnp.where(orders == 0, 1.0, 2.0), 0.0) * (-1.0 / half_turn)
    coef = (phase(orders, out_angles, half_turn) * jnp.concatenate([scale, scale])[:, None]).T
    high, low = split_outside(coef)
    coef = jnp.concatenate([high, high, low], axis=1)

    kept = 2 * pixels
    table = jnp.asarray(sums)

    def cut(start):
        return lax.dynamic_slice_in_dim(table, start + reach, kept, 1)

    tail = cut(1 - kept + correlation[0]) - cut(1 - kept - padding[0])
    head = cut(1 + padding[0]) - cut(1)
    edge = jnp.stack([tail, head], axis=1).reshape(2, 2, half, LANE)
    scalars = jnp.stack([upper, r, correlation[0], blend_width[0]])
    out = filter_rows(
        scalars, x, got, both[0], both[1], flat, dark, first, coef, edge,
        jnp.asarray(gains), jnp.asarray(tw), jnp.asarray(fwd), jnp.asarray(bwd), jnp.asarray(fin),
    )
    return out.reshape(half_block, 1, kept)


def solution(mesh):
    placed = (P("angle", "row", None), P("row", None), P("row", None), P(), P(), P(), P())
    return jax.shard_map(
        local, mesh=mesh, in_specs=placed, out_specs=P("angle", "row", None), check_vma=False
    )
```

profile of v0, /device:TPU:0, one launch (start us, length us, event | category | flops | bytes accessed | tf_op | source)
XLA Modules:
  0.0 134.6 jit_solution(16169153946617594721)
XLA Ops:
  6.5 0.1 fusion.22
  6.6 1.6 %copy-done = f32[128,1,4096]{2,1,0:T(1,128)S(1)} copy-done((f32[128,1,4096]{2,1,0:T(1,128)S(1)}, f32[128,1,4096]{2,1,0:T(1,128)}, u32[]{:S(2)}) %copy-start) | copy-done | bytes 2097176
  8.2 0.7 copy-done.2
  8.9 0.7 copy-done.4
  9.7 2.0 %modes.1 = f32[512,128]{1,0:T(8,128)S(1)} custom-call(f32[4096,128]{1,0:T(8,128)S(1)} %bitcast.31, f32[32,128]{1,0:T(8,128)S(1)} %bitcast.36, f32[32,128]{1,0:T(8,128)S(1)} %bitcast.38, bf16[16,384]{1,0:T(8,128)(2,1)S(1)} %pad_maximum_fusion.4.phi_ref), custom_call_target="tpu_custom_call" | custom-call | flops 50000000 | bytes 3000000 | tf_op jit(solution)/shard_map/modes/pallas_call | solution.py:104
  11.6 0.0 copy-start.11
  11.6 0.9 broadcast_select_fusion
  12.6 1.0 constant_dynamic-slice_fusion
  13.7 3.1 %collective-permute-start = (f32[64,32,128]{2,1,0:T(8,128)}, f32[64,32,128]{2,1,0:T(8,128)S(1)}, u32[]{:S(2)}, u32[]{:S(2)}) collective-permute-start(f32[64,32,128]{2,1,0:T(8,128)} %constant_dynamic-slice_fusion), channel_id=1, source_target_pairs={{0,64},{16,80},{32,96},{48,112},{64,0},{80,16},{96,32},{112,48},{1... | collective-permute-start | bytes 3145736 | tf_op jit(solution)/shard_map/ppermute | solution.py:325
  18.8 0.1 pad_maximum_fusion.7
  18.9 0.1 fusion.20
  19.0 0.1 copy.17
  19.1 0.1 pad_add_fusion.1
  19.2 0.1 pad_maximum_fusion.3.coef_ref
  19.2 0.2 fusion.5
  19.5 0.1 pad_add_fusion.s_ref
  20.2 0.1 pad_maximum_fusion.2.first_ref
  20.4 1.2 subtract_bitcast_fusion
  21.6 80.1 %all-reduce.2.cloned.1.call-done = f32[2,512,128]{2,1,0:T(8,128)} async-done(((f32[2,512,128]{2,1,0:T(8,128)}), f32[2,512,128]{2,1,0:T(8,128)}) %all-reduce.2.cloned.1.call-update) | async-done | bytes 524304 | tf_op jit(solution)/shard_map/psum | solution.py:334
  101.7 1.1 fusion.24
  102.9 0.9 copy-done.6
  103.8 0.9 copy-done.7
  104.8 0.8 copy-done.10
  105.5 22.2 %filter_rows.1 = f32[64,64,128]{2,1,0:T(8,128)} custom-call(s32[4]{0:T(128)S(1)} %pad_add_fusion.s_ref, f32[128,32,128]{2,1,0:T(8,128)S(1)} %bitcast.33, f32[64,32,128]{2,1,0:T(8,128)S(1)} %collective-permute-done.got_ref, f32[16,32,128]{2,1,0:T(8,128)S(1)} %bitcast.35, f32[16,32,128]{2,1,0:T(8,128)S(1)} %bitcast.34, f32[32,128]{1,0:T(8,128)S(1)} %bitcast.37, ...), custom_call_target="tpu_custom_call" | custom-call | flops 10000000000 | bytes 6000000 | tf_op jit(solution)/shard_map/filter_rows/pallas_call | solution.py:291
  (34 shorter events, 0.2 us)
Async XLA Ops:
  6.5 95.2 %all-reduce.2.cloned.1.call-start = ((), (), s32[]{:S(2)}) async-start(), calls=%async_computation | async-start | bytes 1048576 | tf_op jit(solution)/shard_map/psum | solution.py:334
  6.6 1.6 %copy-start = (f32[128,1,4096]{2,1,0:T(1,128)S(1)}, f32[128,1,4096]{2,1,0:T(1,128)}, u32[]{:S(2)}) copy-start(f32[128,1,4096]{2,1,0:T(1,128)} %param.13) | copy-start | bytes 6291460
  8.2 0.7 copy-start.2
  8.9 0.7 copy-start.4
  9.7 2.9 %copy-start.1 = (f32[128,1,4096]{2,1,0:T(1,128)S(1)}, f32[128,1,4096]{2,1,0:T(1,128)}, u32[]{:S(2)}) copy-start(f32[128,1,4096]{2,1,0:T(1,128)} %param.13) | copy-start | bytes 6291460
  11.6 8.7 %copy-start.11 = (f32[2,8192]{1,0:T(2,128)S(1)}, f32[2,8192]{1,0:T(2,128)}, u32[]{:S(2)}) copy-start(f32[2,8192]{1,0:T(2,128)} %constant.148) | copy-start | bytes 196612
  12.6 90.2 %copy-start.3 = (f32[1,4096]{1,0:T(1,128)S(1)}, f32[1,4096]{1,0:T(1,128)}, u32[]{:S(2)}) copy-start(f32[1,4096]{1,0:T(1,128)} %param.14) | copy-start | bytes 49156
  12.6 90.2 %copy-start.5 = (f32[1,4096]{1,0:T(1,128)S(1)}, f32[1,4096]{1,0:T(1,128)}, u32[]{:S(2)}) copy-start(f32[1,4096]{1,0:T(1,128)} %param.15) | copy-start | bytes 49156
  12.6 90.2 %copy-start.8 = (f32[2,64,128]{2,1,0:T(8,128)S(1)}, f32[2,64,128]{2,1,0:T(8,128)}, u32[]{:S(2)}) copy-start(f32[2,64,128]{2,1,0:T(8,128)} %constant.140.clone.tw_ref) | copy-start | bytes 196612
  12.6 90.2 %copy-start.9 = (f32[2,64,128]{2,1,0:T(8,128)S(1)}, f32[2,64,128]{2,1,0:T(8,128)}, u32[]{:S(2)}) copy-start(f32[2,64,128]{2,1,0:T(8,128)} %constant.139.clone.gain_ref) | copy-start | bytes 196612
  13.7 89.1 %collective-permute-start = (f32[64,32,128]{2,1,0:T(8,128)}, f32[64,32,128]{2,1,0:T(8,128)S(1)}, u32[]{:S(2)}, u32[]{:S(2)}) collective-permute-start(f32[64,32,128]{2,1,0:T(8,128)} %constant_dynamic-slice_fusion), channel_id=1, source_target_pairs={{0,64},{16,80},{32,96},{48,112},{64,0},{80,16},{96,32},{112,48},{1... | collective-permute-start | bytes 3145736 | tf_op jit(solution)/shard_map/ppermute | solution.py:325
  102.8 1.0 copy-start.6
  103.8 0.9 copy-start.7
  104.8 0.8 copy-start.10
Sparse Core Ops, SparseCore 0:
  12.7 88.9 all-reduce.1
where the time goes:
time: 135 us
  waiting for transfers between devices  80.1 us (59%)
  Pallas kernels  24.1 us (18%)
  between operations  16.3 us (12%)
  local copies, waits for them, and re-layouts  7.96 us (6%)
  starting transfers between devices  3.11 us (2%)
  other arithmetic  2.96 us (2%)
    psum x1, waiting for transfers between devices, local(): both = lax.psum(slots, 'angle').reshape(2, MODES, blocks, LANE)  80.1 us
    pallas_call x1, Pallas kernels, filter_rows(): pl.pallas_call(main_kernel, out_shape=jax.ShapeDtypeStruct((count, half,...  22.2 us
    unnamed x24, local copies, waits for them, and re-layouts  5.76 us
    ppermute x1, starting transfers between devices, local(): got = lax.ppermute(outgoing, 'angle', pairs)  3.11 us
  transfers between devices with their start and end apart: 2, of which 1 were waited for; matrix products, arithmetic and copies ran while one was open for 3% of the time, Pallas kernels for 0%

commit v1 on v0

v1 whole, which is shorter than its diff:
```python
import functools

import jax
import jax.numpy as jnp
import numpy as np
from jax import lax
from jax.experimental import pallas as pl
from jax.experimental.pallas import tpu as pltpu
from jax.sharding import PartitionSpec as P

KMAX = 8
FCUT = 512
OVL_LO = 512
OVL_HI = 1536
LANE = 128
MODES = 16
GROUP = 4
CHUNK = 8
STACK = 80
MODE_STEP = 2
CORR_STEP = 6
MESH = pl.DeviceIdType.MESH


def split_np(table):
    high = table.astype(jnp.bfloat16)
    low = (table - high.astype(np.float64)).astype(jnp.bfloat16)
    return high, low


def split(value):
    high = value.astype(jnp.bfloat16)
    low = (value - high.astype(jnp.float32)).astype(jnp.bfloat16)
    return high, low


@functools.cache
def constants(length, angle_count, total):
    kept = length // 2
    freq = np.arange(kept, dtype=np.float64)
    ramp = freq / kept * (1.0 + np.cos(np.pi * freq / kept))
    drop = 1.0 - 1.0 / (1.0 + (freq / FCUT) ** 8)
    half = LANE // 2
    gains, sums = [], []
    reach = length * 3 // 4
    for gain in (ramp, ramp * drop):
        full = np.zeros(length)
        full[:kept] = gain
        full[kept + 1 :] = gain[:0:-1]
        kernel = np.fft.ifft(full).real
        offsets = np.arange(-reach, reach + 1)
        table = np.concatenate([[0.0], np.cumsum(kernel[offsets % length])])
        sums.append(np.pad(table, (0, -len(table) % LANE + LANE)).reshape(-1, LANE))
        place = np.arange(length)
        signed = np.where(place < kept, place, place - length)
        turned = kernel * np.exp(-1j * np.pi * signed / length)
        turned[kept] = 0.0
        between = np.fft.fft(turned).real
        k1 = np.arange(half)[:, None]
        k2 = np.arange(LANE)[None, :]
        gains.append(between[k1 + LANE * k2] * (2.0 / length))
    k1 = np.arange(half)[:, None]
    n2 = np.arange(LANE)[None, :]
    turn = 2.0 * np.pi * (k1 + 0.5) * n2 / length
    twiddle = np.stack([np.cos(turn), np.sin(turn)]).astype(np.float32)
    a = np.arange(LANE)[:, None]
    b = np.arange(LANE)[None, :]
    angle = 2.0 * np.pi * (a * b % LANE) / LANE
    c, s = np.cos(angle), np.sin(angle)
    forward = np.concatenate(split_np(np.block([[c, -s], [s, c]])), axis=0)
    backward = np.concatenate(split_np(np.block([[c, s], [-s, c]])), axis=0)
    n1 = np.arange(half)[:, None]
    last = 2.0 * np.pi * ((2 * np.arange(half)[None, :] + 1) * n1 % (2 * LANE)) / (2 * LANE)
    high, low = split_np(np.concatenate([np.cos(last), -np.sin(last)], axis=1))
    final = np.concatenate([high, high, low], axis=1)
    blocks = length // 4 // LANE
    firsts = []
    for q in range((length // 4 - OVL_HI) // LANE, (length // 4 - OVL_LO) // LANE + 1):
        index = np.concatenate([blocks - 1 - np.arange(blocks), q + np.arange(STACK - blocks)])[None, :]
        turn = np.pi * ((2 * k1 + 1) * index % (2 * LANE)) / LANE
        high, low = split_np(np.concatenate([np.cos(turn), -np.sin(turn)], axis=0))
        firsts.append(np.concatenate([high, high, low], axis=1))
    halves = angle_count // 2
    half_turn = angle_count * total // 2
    orders = np.arange(KMAX)[:, None]
    phis, coefs = [], []
    for place in range(angle_count):
        base = place % halves * total
        turn = 2.0 * np.pi * (orders * (base + np.arange(total)[None, :]) % half_turn) / half_turn
        table = np.concatenate([np.cos(turn), np.sin(turn)], axis=0)
        if place < halves:
            high, low = split_np(table)
            phis.append(np.concatenate([high, high, low], axis=1))
        start = place // halves * (total // 2)
        table = table[:, start : start + total // 2] * (-2.0 / half_turn)
        table[0] *= 0.5
        groups = table.reshape(halves, GROUP, -1)
        table = np.concatenate([groups[(place % halves - k) % halves] for k in range(halves)], axis=0)
        high, low = split_np(table.T)
        coefs.append(np.concatenate([high, high, low], axis=1))
    return dict(
        phi=np.concatenate(phis, axis=0),
        first=np.concatenate(firsts, axis=0),
        sums=np.concatenate(sums, axis=0).astype(np.float32),
        gain=np.concatenate(gains, axis=0).astype(np.float32),
        twiddle=twiddle.reshape(2 * half, LANE),
        forward=forward,
        backward=backward,
        final=final,
        coef=np.concatenate(coefs, axis=0),
    )


def dot(a, b):
    return jnp.dot(a, b, preferred_element_type=jnp.float32)


def cut(sums_s, which, start):
    half = LANE // 2
    rows = sums_s.shape[0] // 2
    row = lax.shift_right_logical(start, 7)
    rest = jnp.bitwise_and(start, LANE - 1)
    back = jnp.bitwise_and(LANE - rest, LANE - 1)
    here = pltpu.roll(sums_s[pl.ds(which * rows + row, half), :], back, 1)
    there = pltpu.roll(sums_s[pl.ds(which * rows + row + 1, half), :], back, 1)
    lane = lax.broadcasted_iota(jnp.int32, (half, LANE), 1)
    return jnp.where(lane < LANE - rest, here, there)


NAMES = ("phi", "first", "sums", "gain", "twiddle", "forward", "backward", "final", "coef")


def body_kernel(*refs):
    corr_ref, blend_ref, pad_ref, cutoff_ref, x_ref, flat_ref, dark_ref = refs[:7]
    tables = refs[7 : 7 + len(NAMES)]
    out_ref = refs[7 + len(NAMES)]
    rest = refs[8 + len(NAMES) :]
    held = rest[: len(NAMES)]
    (xs, got_s, gown_s, rs_s, sum_s, gx_s, bg_s, corr_s, edge_t, first_d,
     main_s, back_s, shift_s, yh_s, yl_s, res_s, edge_s,
     tsem, xsem, fsem, dsem, ex_send, ex_recv, rs_send, rs_recv, gx_send, gx_recv, ag_send, ag_recv,
     flat_s, dark_s) = rest[len(NAMES) :]
    phi_s, first_s, sums_s, gain_s, tw_s, fwd_s, bwd_s, fin_s, coef_s = held

    place = lax.axis_index("angle")
    row = lax.axis_index("row")
    halves = GROUP
    yy = lax.rem(place, halves)
    upper = place // halves
    half = LANE // 2
    wide = 2 * LANE
    blocks = flat_ref.shape[0]
    total = xs.shape[0] // blocks
    count = total // 2
    chunks = count // CHUNK
    length = 4 * blocks * LANE
    kept = length // 2
    reach = length * 3 // 4
    partner = (lax.rem(place + halves, 2 * halves), row)
    peers = [(upper * halves + lax.rem(yy + k, halves), row) for k in range(halves)]

    barrier = pltpu.get_barrier_semaphore()
    pl.semaphore_signal(barrier, inc=1, device_id=partner, device_id_type=MESH)
    for k in range(1, halves):
        pl.semaphore_signal(barrier, inc=1, device_id=peers[k], device_id_type=MESH)
    load_x = pltpu.make_async_copy(x_ref, xs, xsem)
    load_x.start()
    load_f = pltpu.make_async_copy(flat_ref, flat_s, fsem)
    load_f.start()
    load_d = pltpu.make_async_copy(dark_ref, dark_s, dsem)
    load_d.start()
    loads = [pltpu.make_async_copy(tables[i], held[i], tsem.at[i]) for i in range(len(NAMES))]
    for load in loads:
        load.start()
    pl.semaphore_wait(barrier, halves)

    span = CHUNK * blocks

    def exchange(c):
        return pltpu.make_async_remote_copy(
            src_ref=x_ref.at[pl.ds((1 - upper) * count * blocks + c * span, span), :],
            dst_ref=got_s.at[pl.ds(c * span, span), :],
            send_sem=ex_send.at[c],
            recv_sem=ex_recv.at[c],
            device_id=partner,
            device_id_type=MESH,
        )

    for c in range(chunks):
        exchange(c).start()

    block = GROUP * blocks

    def scatter(k):
        return pltpu.make_async_remote_copy(
            src_ref=gown_s.at[pl.ds(lax.rem(yy + k, halves) * block, block), :],
            dst_ref=rs_s.at[k],
            send_sem=rs_send.at[k],
            recv_sem=rs_recv.at[k],
            device_id=peers[k],
            device_id_type=MESH,
        )

    def across():
        return pltpu.make_async_remote_copy(
            src_ref=sum_s,
            dst_ref=gx_s,
            send_sem=gx_send,
            recv_sem=gx_recv,
            device_id=partner,
            device_id_type=MESH,
        )

    def gather(k):
        return pltpu.make_async_remote_copy(
            src_ref=bg_s.at[pl.ds(0, GROUP * half), :],
            dst_ref=bg_s.at[pl.ds(k * GROUP * half, GROUP * half), :],
            send_sem=ag_send.at[k],
            recv_sem=ag_recv.at[k],
            device_id=peers[k],
            device_id_type=MESH,
        )

    load_f.wait()
    load_d.wait()
    load_x.wait()
    for load in loads:
        load.wait()

    phi = phi_s[pl.ds(yy * MODES, MODES), :]
    for n1 in range(blocks):
        dark = dark_s[n1 : n1 + 1, :]
        base = jnp.log(flat_s[n1 : n1 + 1, :] - dark)
        rows = xs[pl.ds(n1, total, stride=blocks), :]
        high, low = split(base - jnp.log(rows - dark))
        gown_s[pl.ds(n1, MODES, stride=blocks), :] = dot(phi, jnp.concatenate([high, low, high], axis=0))
    for k in range(1, halves):
        scatter(k).start()

    corr = corr_ref[0]
    pad = pad_ref[0]
    blend = blend_ref[0].astype(jnp.float32)
    shift = blocks * LANE - corr
    q = lax.shift_right_logical(shift, 7)
    roll_by = jnp.bitwise_and(shift, LANE - 1)
    least = blocks - OVL_HI // LANE
    q = jnp.clip(q - least, 0, first_s.shape[0] // LANE - 1)
    first_d[...] = first_s[pl.ds(q * LANE, LANE), :]
    for which in range(2):
        tail = cut(sums_s, which, 1 - kept + corr + reach) - cut(sums_s, which, 1 - kept - pad + reach)
        ahead = cut(sums_s, which, 1 + pad + reach) - cut(sums_s, which, jnp.int32(1 + reach))
        edge_t[which * LANE : which * LANE + half, :] = tail
        edge_t[which * LANE + half : (which + 1) * LANE, :] = ahead
    shift_s[...] = jnp.zeros_like(shift_s)
    pixel = (
        lax.broadcasted_iota(jnp.int32, (blocks, LANE), 0) * LANE
        + lax.broadcasted_iota(jnp.int32, (blocks, LANE), 1)
    ).astype(jnp.float32)

    def step(v, carry):
        is_mode = v == MODE_STEP
        c = v - (v > MODE_STEP).astype(jnp.int32)

        @pl.when(v == MODE_STEP - 1)
        def _():
            for k in range(1, halves):
                scatter(k).wait()
            sum_s[...] = gown_s[pl.ds(yy * block, block), :] + rs_s[1] + rs_s[2] + rs_s[3]
            across().start()

        @pl.when(is_mode)
        def _():
            across().wait()
            mine = sum_s[...].reshape(GROUP, blocks, LANE)
            theirs = gx_s[...].reshape(GROUP, blocks, LANE)
            main_s[:GROUP] = jnp.where(upper == 1, theirs, mine)
            back_s[:GROUP] = jnp.where(upper == 1, mine, theirs)

        @pl.when(v == CORR_STEP)
        def _():
            for k in range(1, halves):
                gather(k).wait()
            coef = coef_s[pl.ds(place * count, count), :]
            for n1 in range(half):
                high, low = split(bg_s[pl.ds(n1, MODES, stride=half), :])
                corr_s[pl.ds(n1, count, stride=half), :] = dot(coef, jnp.concatenate([high, low, high], axis=0))

        @pl.when(jnp.logical_not(is_mode))
        def _():
            exchange(c).wait()
            dark = dark_s[...]
            base = jnp.log(flat_s[...] - dark)
            own = xs[pl.ds(upper * count * blocks + c * span, span), :].reshape(CHUNK, blocks, LANE)
            own = base - jnp.log(own - dark)
            got = base - jnp.log(got_s[pl.ds(c * span, span), :].reshape(CHUNK, blocks, LANE) - dark)
            main_s[...] = jnp.where(upper == 1, got, own)
            back_s[...] = jnp.where(upper == 1, own, got)

        weight = jnp.clip((pixel + 0.5 - corr.astype(jnp.float32) * 0.5) / blend + 0.5, 0.0, 1.0)
        lanes = lax.broadcasted_iota(jnp.int32, (blocks, LANE), 1)
        lanes48 = lax.broadcasted_iota(jnp.int32, (STACK - blocks, LANE), 1)
        for t in range(0, CHUNK, 2):
            parts = []
            for i in (t, t + 1):
                main = main_s[i]
                back = back_s[i]
                edge_s[0, i : i + 1, :] = jnp.broadcast_to(main[blocks - 1 : blocks, LANE - 1 :], (1, LANE))
                edge_s[1, i : i + 1, :] = jnp.broadcast_to(back[blocks - 1 : blocks, LANE - 1 :], (1, LANE))
                left = jnp.take_along_axis(back * weight, LANE - 1 - lanes, axis=1)
                shift_s[i, 8 : 8 + blocks, :] = pltpu.roll(main * weight, roll_by, 1)
                here = shift_s[i, 8 : 8 + STACK - blocks, :]
                prev = shift_s[i, 7 : 7 + STACK - blocks, :]
                right = jnp.where(lanes48 >= roll_by, here, prev)
                parts.append(jnp.concatenate([left, right], axis=0))
            high, low = split(jnp.concatenate(parts, axis=1))
            y = dot(first_d[...], jnp.concatenate([high, low, high], axis=0))
            cos, sin = tw_s[:half, :], tw_s[half:, :]
            for j, i in enumerate((t, t + 1)):
                re = y[:half, j * LANE : (j + 1) * LANE]
                im = y[half:, j * LANE : (j + 1) * LANE]
                turned = jnp.concatenate([re * cos + im * sin, im * cos - re * sin], axis=1)
                high, low = split(turned)
                yh_s[i * half : (i + 1) * half, :] = high
                yl_s[i * half : (i + 1) * half, :] = low
        which = is_mode.astype(jnp.int32)
        gain = gain_s[pl.ds(which * half, half), :]
        tail = edge_t[pl.ds(which * LANE, half), :]
        ahead = edge_t[pl.ds(which * LANE + half, half), :]
        gain2 = jnp.concatenate([gain, gain], axis=1)
        for t in range(0, CHUNK, 2):
            rows = slice(t * half, (t + 2) * half)
            z = (
                dot(yh_s[rows, :], fwd_s[:wide, :])
                + dot(yl_s[rows, :], fwd_s[:wide, :])
                + dot(yh_s[rows, :], fwd_s[wide:, :])
            )
            z = z * jnp.concatenate([gain2, gain2], axis=0)
            high, low = split(z)
            u = dot(high, bwd_s[:wide, :]) + dot(low, bwd_s[:wide, :]) + dot(high, bwd_s[wide:, :])
            parts = []
            cos, sin = tw_s[:half, :], tw_s[half:, :]
            for j in range(2):
                re = u[j * half : (j + 1) * half, :LANE]
                im = u[j * half : (j + 1) * half, LANE:]
                parts.append(jnp.concatenate([re * cos - im * sin, im * cos + re * sin], axis=0))
            high, low = split(jnp.concatenate(parts, axis=1))
            o = dot(fin_s[...], jnp.concatenate([high, low, high], axis=0))
            for j in range(2):
                i = t + j
                res_s[i] = (
                    o[:, j * LANE : (j + 1) * LANE]
                    + edge_s[0, i : i + 1, :] * tail
                    + edge_s[1, i : i + 1, :] * ahead
                )

        @pl.when(is_mode)
        def _():
            for i in range(GROUP):
                order = jnp.bitwise_and(yy * GROUP + i, KMAX - 1)
                keep = jnp.where(order < cutoff_ref[0], 1.0, 0.0)
                bg_s[i * half : (i + 1) * half, :] = res_s[i] * keep
            for k in range(1, halves):
                gather(k).start()

        @pl.when(jnp.logical_not(is_mode))
        def _():
            out_ref[pl.ds(c * CHUNK, CHUNK)] = res_s[...]

        return carry

    lax.fori_loop(0, chunks + 1, step, 0)

    def finish(i, carry):
        out_ref[i] = out_ref[i] + corr_s[pl.ds(i * half, half), :]
        return carry

    lax.fori_loop(0, count, finish, 0)


def local(intensity, flat_field, dark_field, correlation, blend_width, padding, cutoff):
    angle_count = lax.axis_size("angle")
    total = intensity.shape[0]
    count = total // 2
    pixels = intensity.shape[2]
    length = 4 * pixels
    blocks = pixels // LANE
    half = LANE // 2
    tables = constants(length, angle_count, total)
    tables = [jnp.asarray(tables[name]) for name in NAMES]
    block = GROUP * blocks
    peers = angle_count // 2
    f32, bf16 = jnp.float32, jnp.bfloat16
    dma = pltpu.SemaphoreType.DMA
    scratch = [pltpu.VMEM(t.shape, t.dtype) for t in tables] + [
        pltpu.VMEM((total * blocks, LANE), f32),
        pltpu.VMEM((count * blocks, LANE), f32),
        pltpu.VMEM((MODES * blocks, LANE), f32),
        pltpu.VMEM((peers, block, LANE), f32),
        pltpu.VMEM((block, LANE), f32),
        pltpu.VMEM((block, LANE), f32),
        pltpu.VMEM((MODES * half, LANE), f32),
        pltpu.VMEM((count * half, LANE), f32),
        pltpu.VMEM((4 * half, LANE), f32),
        pltpu.VMEM((LANE, 3 * STACK), bf16),
        pltpu.VMEM((CHUNK, blocks, LANE), f32),
        pltpu.VMEM((CHUNK, blocks, LANE), f32),
        pltpu.VMEM((CHUNK, STACK - blocks + 8, LANE), f32),
        pltpu.VMEM((CHUNK * half, 2 * LANE), bf16),
        pltpu.VMEM((CHUNK * half, 2 * LANE), bf16),
        pltpu.VMEM((CHUNK, half, LANE), f32),
        pltpu.VMEM((2, CHUNK, LANE), f32),
        dma((len(tables),)),
        dma,
        dma,
        dma,
        dma((count // CHUNK,)),
        dma((count // CHUNK,)),
        dma((peers,)),
        dma((peers,)),
        dma,
        dma,
        dma((peers,)),
        dma((peers,)),
        pltpu.VMEM((blocks, LANE), f32),
        pltpu.VMEM((blocks, LANE), f32),
    ]
    out = pl.pallas_call(
        body_kernel,
        out_shape=jax.ShapeDtypeStruct((count, half, LANE), f32),
        in_specs=[pl.BlockSpec(memory_space=pltpu.SMEM)] * 4
        + [pl.BlockSpec(memory_space=pl.ANY)] * (3 + len(tables)),
        out_specs=pl.BlockSpec(memory_space=pltpu.VMEM),
        scratch_shapes=scratch,
        compiler_params=pltpu.CompilerParams(
            vmem_limit_bytes=56 << 20, collective_id=0, has_side_effects=True
        ),
        name="filter_rows",
    )(
        correlation,
        blend_width,
        padding,
        cutoff,
        intensity.reshape(total * blocks, LANE),
        flat_field.reshape(blocks, LANE),
        dark_field.reshape(blocks, LANE),
        *tables,
    )
    return out.reshape(count, 1, 2 * pixels)


def solution(mesh):
    placed = (P("angle", "row", None), P("row", None), P("row", None), P(), P(), P(), P())
    return jax.shard_map(
        local, mesh=mesh, in_specs=placed, out_specs=P("angle", "row", None), check_vma=False
    )
```

time: 135 us -> 55 us (0.41)
  waiting for transfers between devices: 80.1 us -> 0 us
  Pallas kernels: 24.1 us -> 49.1 us
  between operations: 16.3 us -> 2.59 us
  local copies, waits for them, and re-layouts: 7.96 us -> 3.16 us
  starting transfers between devices: 3.11 us -> 0 us
  other arithmetic: 2.96 us -> 0 us
    psum x1 -> x0, waiting for transfers between devices: 80.1 us -> none  [local(): both = lax.psum(slots, 'angle').reshape(2, MODES, blocks, LANE)]
    pallas_call x2 -> x1, Pallas kernels: 24.1 us -> 49.1 us  [local(): pl.pallas_call(body_kernel, out_shape=jax.ShapeDtypeStruct((count, half,...]
    ppermute x1 -> x0, starting transfers between devices: 3.11 us -> none  [local(): got = lax.ppermute(outgoing, 'angle', pairs)]
    unnamed x24 -> x1, local copies, waits for them, and re-layouts: 5.76 us -> 3.16 us
  transfers between devices with their start and end apart: 2 -> 0, of which waited for: 1 -> 0; matrix products, arithmetic and copies ran while one was open for 3% -> 0% of each run, Pallas kernels for 0% -> 0%
where the time goes in v1:
time: 55 us; the launch traced here: 54.8 us
  Pallas kernels  49.1 us (89%)
  local copies, waits for them, and re-layouts  3.16 us (6%)
  between operations  2.59 us (5%)
    pallas_call x1, Pallas kernels, local(): pl.pallas_call(body_kernel, out_shape=jax.ShapeDtypeStruct((count, half,...  49.1 us
    unnamed x1, local copies, waits for them, and re-layouts  3.16 us

profile of v1, /device:TPU:0, one launch (start us, length us, event | category | flops | bytes accessed | tf_op | source)
XLA Modules:
  0.0 54.8 jit_solution(4118259796297704185)
XLA Ops:
  2.6 49.1 %filter_rows.1 = f32[64,64,128]{2,1,0:T(8,128)} custom-call(s32[1]{0:T(128)S(6)} %copy.19.refs_0_, s32[1]{0:T(128)S(6)} %copy.20.refs_1_, s32[1]{0:T(128)S(6)} %copy.21.refs_2_, s32[1]{0:T(128)S(6)} %copy.22.refs_3_, f32[4096,128]{1,0:T(8,128)} %bitcast.5, f32[32,128]{1,0:T(8,128)} %bitcast.6, f32[32,128]{1,0:T(8,128)} %bitcast.7, ...), custom_call_target="tpu_custom_call" | custom-call | tf_op jit(solution)/shard_map/filter_rows/pallas_call | solution.py:427
  51.7 3.2 %copy.23 = f32[64,1,8192]{2,1,0:T(1,128)} copy(f32[64,1,8192]{2,1,0:T(1,128)} %bitcast.4) | data formatting | bytes 4194304

commit v2 on v1

--- a/solution.py
+++ b/solution.py
@@ -17,8 +17,10 @@
 GROUP = 4
 CHUNK = 8
 STACK = 80
-MODE_STEP = 2
-CORR_STEP = 6
+SUM_STEP = 1
+MODE_STEP = 3
+CORR_STEP = 7
+AHEAD = 2
 MESH = pl.DeviceIdType.MESH
 
 
@@ -186,7 +188,7 @@
             device_id_type=MESH,
         )
 
-    for c in range(chunks):
+    for c in range(AHEAD):
         exchange(c).start()
 
     block = GROUP * blocks
@@ -261,7 +263,7 @@
         is_mode = v == MODE_STEP
         c = v - (v > MODE_STEP).astype(jnp.int32)
 
-        @pl.when(v == MODE_STEP - 1)
+        @pl.when(v == SUM_STEP)
         def _():
             for k in range(1, halves):
                 scatter(k).wait()
@@ -285,9 +287,20 @@
                 high, low = split(bg_s[pl.ds(n1, MODES, stride=half), :])
                 corr_s[pl.ds(n1, count, stride=half), :] = dot(coef, jnp.concatenate([high, low, high], axis=0))
 
+            def mend(i, carry):
+                out_ref[i] = out_ref[i] + corr_s[pl.ds(i * half, half), :]
+                return carry
+
+            lax.fori_loop(0, (CORR_STEP - 1) * CHUNK, mend, 0)
+
         @pl.when(jnp.logical_not(is_mode))
         def _():
             exchange(c).wait()
+
+            @pl.when(c + AHEAD < chunks)
+            def _():
+                exchange(c + AHEAD).start()
+
             dark = dark_s[...]
             base = jnp.log(flat_s[...] - dark)
             own = xs[pl.ds(upper * count * blocks + c * span, span), :].reshape(CHUNK, blocks, LANE)
@@ -362,19 +375,18 @@
             for k in range(1, halves):
                 gather(k).start()
 
-        @pl.when(jnp.logical_not(is_mode))
+        @pl.when(jnp.logical_and(jnp.logical_not(is_mode), v < CORR_STEP))
         def _():
             out_ref[pl.ds(c * CHUNK, CHUNK)] = res_s[...]
 
+        @pl.when(v >= CORR_STEP)
+        def _():
+            rows = corr_s[pl.ds(c * CHUNK * half, CHUNK * half), :]
+            out_ref[pl.ds(c * CHUNK, CHUNK)] = res_s[...] + rows.reshape(CHUNK, half, LANE)
+
         return carry
 
     lax.fori_loop(0, chunks + 1, step, 0)
-
-    def finish(i, carry):
-        out_ref[i] = out_ref[i] + corr_s[pl.ds(i * half, half), :]
-        return carry
-
-    lax.fori_loop(0, count, finish, 0)
 
 
 def local(intensity, flat_field, dark_field, correlation, blend_width, padding, cutoff):
@@ -428,11 +440,11 @@
         body_kernel,
         out_shape=jax.ShapeDtypeStruct((count, half, LANE), f32),
         in_specs=[pl.BlockSpec(memory_space=pltpu.SMEM)] * 4
-        + [pl.BlockSpec(memory_space=pl.ANY)] * (3 + len(tables)),
+        + [pl.BlockSpec(memory_space=pltpu.HBM)] * (3 + len(tables)),
         out_specs=pl.BlockSpec(memory_space=pltpu.VMEM),
         scratch_shapes=scratch,
         compiler_params=pltpu.CompilerParams(
-            vmem_limit_bytes=56 << 20, collective_id=0, has_side_effects=True
+            vmem_limit_bytes=20 << 20, collective_id=0, has_side_effects=True
         ),
         name="filter_rows",
     )(
@@ -440,10 +452,15 @@
         blend_width,
         padding,
         cutoff,
-        intensity.reshape(total * blocks, LANE),
-        flat_field.reshape(blocks, LANE),
-        dark_field.reshape(blocks, LANE),
-        *tables,
+        *[
+            pltpu.with_memory_space_constraint(a, pltpu.HBM)
+            for a in (
+                intensity.reshape(total * blocks, LANE),
+                flat_field.reshape(blocks, LANE),
+                dark_field.reshape(blocks, LANE),
+                *tables,
+            )
+        ],
     )
     return out.reshape(count, 1, 2 * pixels)
 

time: 55 us -> 39.5 us (0.72)
  Pallas kernels: 49.1 us -> 35.5 us
  local copies, waits for them, and re-layouts: 3.16 us -> 1.32 us
    pallas_call x1, Pallas kernels: 49.1 us -> 35.5 us  [local(): pl.pallas_call(body_kernel, out_shape=jax.ShapeDtypeStruct((count, half,...]
    unnamed x1, local copies, waits for them, and re-layouts: 3.16 us -> 1.32 us
where the time goes in v2:
time: 39.5 us; the launch traced here: 39.4 us
  Pallas kernels  35.5 us (90%)
  between operations  2.59 us (7%)
  local copies, waits for them, and re-layouts  1.32 us (3%)
    pallas_call x1, Pallas kernels, local(): pl.pallas_call(body_kernel, out_shape=jax.ShapeDtypeStruct((count, half,...  35.5 us
    unnamed x1, local copies, waits for them, and re-layouts  1.32 us

profile of v2, /device:TPU:0, one launch (start us, length us, event | category | flops | bytes accessed | tf_op | source)
XLA Modules:
  0.0 39.4 jit_solution(17288640149536300266)
XLA Ops:
  2.6 35.5 %filter_rows.1 = f32[64,64,128]{2,1,0:T(8,128)S(1)} custom-call(s32[1]{0:T(128)S(6)} %copy.19.refs_0_, s32[1]{0:T(128)S(6)} %copy.20.refs_1_, s32[1]{0:T(128)S(6)} %copy.21.refs_2_, s32[1]{0:T(128)S(6)} %copy.22.refs_3_, f32[4096,128]{1,0:T(8,128)} %bitcast.5, f32[32,128]{1,0:T(8,128)} %bitcast.6, f32[32,128]{1,0:T(8,128)} %bitcast.7, ...), custom_call_target="tpu_custom_call" | custom-call | tf_op jit(solution)/shard_map/filter_rows/pallas_call | solution.py:439
  38.0 1.3 %copy.23 = f32[64,1,8192]{2,1,0:T(1,128)} copy(f32[64,1,8192]{2,1,0:T(1,128)S(1)} %bitcast.4) | data formatting | bytes 4194304

commit v3 on v2

--- a/solution.py
+++ b/solution.py
@@ -19,8 +19,9 @@
 STACK = 80
 SUM_STEP = 1
 MODE_STEP = 3
-CORR_STEP = 7
-AHEAD = 2
+CORR_STEP = 6
+FIRST = 3
+AHEAD = 4
 MESH = pl.DeviceIdType.MESH
 
 
@@ -69,8 +70,10 @@
     b = np.arange(LANE)[None, :]
     angle = 2.0 * np.pi * (a * b % LANE) / LANE
     c, s = np.cos(angle), np.sin(angle)
-    forward = np.concatenate(split_np(np.block([[c, -s], [s, c]])), axis=0)
-    backward = np.concatenate(split_np(np.block([[c, s], [-s, c]])), axis=0)
+    high, low = split_np(np.block([[c, -s], [s, c]]))
+    forward = np.concatenate([high, high, low], axis=0)
+    high, low = split_np(np.block([[c, s], [-s, c]]))
+    backward = np.concatenate([high, high, low], axis=0)
     n1 = np.arange(half)[:, None]
     last = 2.0 * np.pi * ((2 * np.arange(half)[None, :] + 1) * n1 % (2 * LANE)) / (2 * LANE)
     high, low = split_np(np.concatenate([np.cos(last), -np.sin(last)], axis=1))
@@ -129,20 +132,57 @@
     return jnp.where(lane < LANE - rest, here, there)
 
 
-NAMES = ("phi", "first", "sums", "gain", "twiddle", "forward", "backward", "final", "coef")
+SCRATCH_NAMES = ("phi", "first", "sums", "gain", "forward", "coef")
+NAMES = SCRATCH_NAMES + ("twiddle", "backward", "final")
+
+
+def inverse(zk_s, bwd_s, fin_s, tw_s, uk_s):
+    half = LANE // 2
+    u = dot(zk_s[...], bwd_s[...])
+    cos, sin = tw_s[:half, :], tw_s[half:, :]
+    for i in range(CHUNK):
+        re = u[i * half : (i + 1) * half, :LANE]
+        im = u[i * half : (i + 1) * half, LANE:]
+        high, low = split(jnp.concatenate([re * cos - im * sin, im * cos + re * sin], axis=0))
+        cols = slice(i * LANE, (i + 1) * LANE)
+        uk_s[:LANE, cols] = high
+        uk_s[LANE : 2 * LANE, cols] = low
+        uk_s[2 * LANE :, cols] = high
+    return dot(fin_s[...], uk_s[...])
+
+
+def finish_kernel(out_ref, zk_ref, bias_ref, bwd_ref, fin_ref, tw_ref, y_ref, uk_s, res_s, sems):
+    done = out_ref.shape[0]
+    part = done // (sems.shape[0] - 1)
+    copies = [
+        pltpu.make_async_copy(
+            out_ref.at[pl.ds(i * part, part)], y_ref.at[pl.ds(i * part, part)], sems.at[i]
+        )
+        for i in range(done // part)
+    ]
+    for copy in copies:
+        copy.start()
+    o = inverse(zk_ref, bwd_ref, fin_ref, tw_ref, uk_s)
+    for i in range(CHUNK):
+        res_s[i] = o[:, i * LANE : (i + 1) * LANE] + bias_ref[i]
+    last = pltpu.make_async_copy(res_s, y_ref.at[pl.ds(done, CHUNK)], sems.at[done // part])
+    last.start()
+    for copy in copies:
+        copy.wait()
+    last.wait()
 
 
 def body_kernel(*refs):
-    corr_ref, blend_ref, pad_ref, cutoff_ref, x_ref, flat_ref, dark_ref = refs[:7]
+    scalar_refs, (x_ref, flat_ref, dark_ref) = refs[:4], refs[4:7]
     tables = refs[7 : 7 + len(NAMES)]
-    out_ref = refs[7 + len(NAMES)]
-    rest = refs[8 + len(NAMES) :]
-    held = rest[: len(NAMES)]
+    out_ref, zk_o, bias_o, bwd_s, fin_s, tw_s = refs[7 + len(NAMES) : 13 + len(NAMES)]
+    rest = refs[13 + len(NAMES) :]
     (xs, got_s, gown_s, rs_s, sum_s, gx_s, bg_s, corr_s, edge_t, first_d,
-     main_s, back_s, shift_s, yh_s, yl_s, res_s, edge_s,
+     main_s, back_s, shift_s, xk_s, yk_s, zk_s, uk_s, res_s, edge_s,
      tsem, xsem, fsem, dsem, ex_send, ex_recv, rs_send, rs_recv, gx_send, gx_recv, ag_send, ag_recv,
-     flat_s, dark_s) = rest[len(NAMES) :]
-    phi_s, first_s, sums_s, gain_s, tw_s, fwd_s, bwd_s, fin_s, coef_s = held
+     flat_s, dark_s) = rest[len(SCRATCH_NAMES) :]
+    phi_s, first_s, sums_s, gain_s, fwd_s, coef_s = rest[: len(SCRATCH_NAMES)]
+    held = (phi_s, first_s, sums_s, gain_s, fwd_s, coef_s, tw_s, bwd_s, fin_s)
 
     place = lax.axis_index("angle")
     row = lax.axis_index("row")
@@ -172,8 +212,7 @@
     load_d = pltpu.make_async_copy(dark_ref, dark_s, dsem)
     load_d.start()
     loads = [pltpu.make_async_copy(tables[i], held[i], tsem.at[i]) for i in range(len(NAMES))]
-    for load in loads:
-        load.start()
+    corr_ref, blend_ref, pad_ref, cutoff_ref = scalar_refs
     pl.semaphore_wait(barrier, halves)
 
     span = CHUNK * blocks
@@ -188,8 +227,10 @@
             device_id_type=MESH,
         )
 
-    for c in range(AHEAD):
+    for c in range(FIRST):
         exchange(c).start()
+    for load in loads:
+        load.start()
 
     block = GROUP * blocks
 
@@ -259,6 +300,65 @@
         + lax.broadcasted_iota(jnp.int32, (blocks, LANE), 1)
     ).astype(jnp.float32)
 
+    def receive(c):
+        exchange(c).wait()
+
+        @pl.when(False if isinstance(c, int) else jnp.logical_and(c >= SUM_STEP, c + AHEAD < chunks))
+        def _():
+            exchange(c + AHEAD).start()
+
+        dark = dark_s[...]
+        base = jnp.log(flat_s[...] - dark)
+        own = xs[pl.ds(upper * count * blocks + c * span, span), :].reshape(CHUNK, blocks, LANE)
+        own = base - jnp.log(own - dark)
+        got = base - jnp.log(got_s[pl.ds(c * span, span), :].reshape(CHUNK, blocks, LANE) - dark)
+        main_s[...] = jnp.where(upper == 1, got, own)
+        back_s[...] = jnp.where(upper == 1, own, got)
+
+    def front(which, zk_s):
+        weight = jnp.clip((pixel + 0.5 - corr.astype(jnp.float32) * 0.5) / blend + 0.5, 0.0, 1.0)
+        lanes = lax.broadcasted_iota(jnp.int32, (blocks, LANE), 1)
+        lanes48 = lax.broadcasted_iota(jnp.int32, (STACK - blocks, LANE), 1)
+        for i in range(CHUNK):
+            main = main_s[i]
+            back = back_s[i]
+            edge_s[0, i : i + 1, :] = jnp.broadcast_to(main[blocks - 1 : blocks, LANE - 1 :], (1, LANE))
+            edge_s[1, i : i + 1, :] = jnp.broadcast_to(back[blocks - 1 : blocks, LANE - 1 :], (1, LANE))
+            left = jnp.take_along_axis(back * weight, LANE - 1 - lanes, axis=1)
+            shift_s[i, 8 : 8 + blocks, :] = pltpu.roll(main * weight, roll_by, 1)
+            here = shift_s[i, 8 : 8 + STACK - blocks, :]
+            prev = shift_s[i, 7 : 7 + STACK - blocks, :]
+            right = jnp.where(lanes48 >= roll_by, here, prev)
+            high, low = split(jnp.concatenate([left, right], axis=0))
+            cols = slice(i * LANE, (i + 1) * LANE)
+            xk_s[:STACK, cols] = high
+            xk_s[STACK : 2 * STACK, cols] = low
+            xk_s[2 * STACK :, cols] = high
+        y = dot(first_d[...], xk_s[...])
+        cos, sin = tw_s[:half, :], tw_s[half:, :]
+        for i in range(CHUNK):
+            re = y[:half, i * LANE : (i + 1) * LANE]
+            im = y[half:, i * LANE : (i + 1) * LANE]
+            high, low = split(jnp.concatenate([re * cos + im * sin, im * cos - re * sin], axis=1))
+            rows = slice(i * half, (i + 1) * half)
+            yk_s[rows, :wide] = high
+            yk_s[rows, wide : 2 * wide] = low
+            yk_s[rows, 2 * wide :] = high
+        gain = gain_s[pl.ds(which * half, half), :]
+        gain2 = jnp.concatenate([gain, gain], axis=1)
+        z = dot(yk_s[...], fwd_s[...])
+        for i in range(CHUNK):
+            rows = slice(i * half, (i + 1) * half)
+            high, low = split(z[rows] * gain2)
+            zk_s[rows, :wide] = high
+            zk_s[rows, wide : 2 * wide] = low
+            zk_s[rows, 2 * wide :] = high
+
+    def edges(which, i):
+        tail = edge_t[pl.ds(which * LANE, half), :]
+        ahead = edge_t[pl.ds(which * LANE + half, half), :]
+        return edge_s[0, i : i + 1, :] * tail + edge_s[1, i : i + 1, :] * ahead
+
     def step(v, carry):
         is_mode = v == MODE_STEP
         c = v - (v > MODE_STEP).astype(jnp.int32)
@@ -269,6 +369,8 @@
                 scatter(k).wait()
             sum_s[...] = gown_s[pl.ds(yy * block, block), :] + rs_s[1] + rs_s[2] + rs_s[3]
             across().start()
+            for c in range(FIRST, AHEAD + SUM_STEP):
+                exchange(c).start()
 
         @pl.when(is_mode)
         def _():
@@ -283,9 +385,12 @@
             for k in range(1, halves):
                 gather(k).wait()
             coef = coef_s[pl.ds(place * count, count), :]
-            for n1 in range(half):
-                high, low = split(bg_s[pl.ds(n1, MODES, stride=half), :])
-                corr_s[pl.ds(n1, count, stride=half), :] = dot(coef, jnp.concatenate([high, low, high], axis=0))
+            for n1 in range(0, half, 2):
+                pair = [bg_s[pl.ds(n1 + j, MODES, stride=half), :] for j in range(2)]
+                high, low = split(jnp.concatenate(pair, axis=1))
+                fix = dot(coef, jnp.concatenate([high, low, high], axis=0))
+                for j in range(2):
+                    corr_s[pl.ds(n1 + j, count, stride=half), :] = fix[:, j * LANE : (j + 1) * LANE]
 
             def mend(i, carry):
                 out_ref[i] = out_ref[i] + corr_s[pl.ds(i * half, half), :]
@@ -295,76 +400,13 @@
 
         @pl.when(jnp.logical_not(is_mode))
         def _():
-            exchange(c).wait()
-
-            @pl.when(c + AHEAD < chunks)
-            def _():
-                exchange(c + AHEAD).start()
-
-            dark = dark_s[...]
-            base = jnp.log(flat_s[...] - dark)
-            own = xs[pl.ds(upper * count * blocks + c * span, span), :].reshape(CHUNK, blocks, LANE)
-            own = base - jnp.log(own - dark)
-            got = base - jnp.log(got_s[pl.ds(c * span, span), :].reshape(CHUNK, blocks, LANE) - dark)
-            main_s[...] = jnp.where(upper == 1, got, own)
-            back_s[...] = jnp.where(upper == 1, own, got)
-
-        weight = jnp.clip((pixel + 0.5 - corr.astype(jnp.float32) * 0.5) / blend + 0.5, 0.0, 1.0)
-        lanes = lax.broadcasted_iota(jnp.int32, (blocks, LANE), 1)
-        lanes48 = lax.broadcasted_iota(jnp.int32, (STACK - blocks, LANE), 1)
-        for t in range(0, CHUNK, 2):
-            parts = []
-            for i in (t, t + 1):
-                main = main_s[i]
-                back = back_s[i]
-                edge_s[0, i : i + 1, :] = jnp.broadcast_to(main[blocks - 1 : blocks, LANE - 1 :], (1, LANE))
-                edge_s[1, i : i + 1, :] = jnp.broadcast_to(back[blocks - 1 : blocks, LANE - 1 :], (1, LANE))
-                left = jnp.take_along_axis(back * weight, LANE - 1 - lanes, axis=1)
-                shift_s[i, 8 : 8 + blocks, :] = pltpu.roll(main * weight, roll_by, 1)
-                here = shift_s[i, 8 : 8 + STACK - blocks, :]
-                prev = shift_s[i, 7 : 7 + STACK - blocks, :]
-                right = jnp.where(lanes48 >= roll_by, here, prev)
-                parts.append(jnp.concatenate([left, right], axis=0))
-            high, low = split(jnp.concatenate(parts, axis=1))
-            y = dot(first_d[...], jnp.concatenate([high, low, high], axis=0))
-            cos, sin = tw_s[:half, :], tw_s[half:, :]
-            for j, i in enumerate((t, t + 1)):
-                re = y[:half, j * LANE : (j + 1) * LANE]
-                im = y[half:, j * LANE : (j + 1) * LANE]
-                turned = jnp.concatenate([re * cos + im * sin, im * cos - re * sin], axis=1)
-                high, low = split(turned)
-                yh_s[i * half : (i + 1) * half, :] = high
-                yl_s[i * half : (i + 1) * half, :] = low
+            receive(c)
+
         which = is_mode.astype(jnp.int32)
-        gain = gain_s[pl.ds(which * half, half), :]
-        tail = edge_t[pl.ds(which * LANE, half), :]
-        ahead = edge_t[pl.ds(which * LANE + half, half), :]
-        gain2 = jnp.concatenate([gain, gain], axis=1)
-        for t in range(0, CHUNK, 2):
-            rows = slice(t * half, (t + 2) * half)
-            z = (
-                dot(yh_s[rows, :], fwd_s[:wide, :])
-                + dot(yl_s[rows, :], fwd_s[:wide, :])
-                + dot(yh_s[rows, :], fwd_s[wide:, :])
-            )
-            z = z * jnp.concatenate([gain2, gain2], axis=0)
-            high, low = split(z)
-            u = dot(high, bwd_s[:wide, :]) + dot(low, bwd_s[:wide, :]) + dot(high, bwd_s[wide:, :])
-            parts = []
-            cos, sin = tw_s[:half, :], tw_s[half:, :]
-            for j in range(2):
-                re = u[j * half : (j + 1) * half, :LANE]
-                im = u[j * half : (j + 1) * half, LANE:]
-                parts.append(jnp.concatenate([re * cos - im * sin, im * cos + re * sin], axis=0))
-            high, low = split(jnp.concatenate(parts, axis=1))
-            o = dot(fin_s[...], jnp.concatenate([high, low, high], axis=0))
-            for j in range(2):
-                i = t + j
-                res_s[i] = (
-                    o[:, j * LANE : (j + 1) * LANE]
-                    + edge_s[0, i : i + 1, :] * tail
-                    + edge_s[1, i : i + 1, :] * ahead
-                )
+        front(which, zk_s)
+        o = inverse(zk_s, bwd_s, fin_s, tw_s, uk_s)
+        for i in range(CHUNK):
+            res_s[i] = o[:, i * LANE : (i + 1) * LANE] + edges(which, i)
 
         @pl.when(is_mode)
         def _():
@@ -386,7 +428,13 @@
 
         return carry
 
-    lax.fori_loop(0, chunks + 1, step, 0)
+    lax.fori_loop(0, chunks, step, 0)
+    for i in range(CHUNK):
+        bias_o[i] = corr_s[((chunks - 1) * CHUNK + i) * half : ((chunks - 1) * CHUNK + i + 1) * half, :]
+    receive(chunks - 1)
+    front(0, zk_o)
+    for i in range(CHUNK):
+        bias_o[i] = bias_o[i] + edges(0, i)
 
 
 def local(intensity, flat_field, dark_field, correlation, blend_width, padding, cutoff):
@@ -403,7 +451,7 @@
     peers = angle_count // 2
     f32, bf16 = jnp.float32, jnp.bfloat16
     dma = pltpu.SemaphoreType.DMA
-    scratch = [pltpu.VMEM(t.shape, t.dtype) for t in tables] + [
+    scratch = [pltpu.VMEM(t.shape, t.dtype) for t in tables[: len(SCRATCH_NAMES)]] + [
         pltpu.VMEM((total * blocks, LANE), f32),
         pltpu.VMEM((count * blocks, LANE), f32),
         pltpu.VMEM((MODES * blocks, LANE), f32),
@@ -417,8 +465,10 @@
         pltpu.VMEM((CHUNK, blocks, LANE), f32),
         pltpu.VMEM((CHUNK, blocks, LANE), f32),
         pltpu.VMEM((CHUNK, STACK - blocks + 8, LANE), f32),
-        pltpu.VMEM((CHUNK * half, 2 * LANE), bf16),
-        pltpu.VMEM((CHUNK * half, 2 * LANE), bf16),
+        pltpu.VMEM((3 * STACK, CHUNK * LANE), bf16),
+        pltpu.VMEM((CHUNK * half, 6 * LANE), bf16),
+        pltpu.VMEM((CHUNK * half, 6 * LANE), bf16),
+        pltpu.VMEM((3 * LANE, CHUNK * LANE), bf16),
         pltpu.VMEM((CHUNK, half, LANE), f32),
         pltpu.VMEM((2, CHUNK, LANE), f32),
         dma((len(tables),)),
@@ -436,12 +486,18 @@
         pltpu.VMEM((blocks, LANE), f32),
         pltpu.VMEM((blocks, LANE), f32),
     ]
-    out = pl.pallas_call(
+    shape = jax.ShapeDtypeStruct
+    outs = [
+        shape((count - CHUNK, half, LANE), f32),
+        shape((CHUNK * half, 6 * LANE), bf16),
+        shape((CHUNK, half, LANE), f32),
+    ] + [shape(tables[NAMES.index(name)].shape, tables[NAMES.index(name)].dtype) for name in ("backward", "final", "twiddle")]
+    parts = pl.pallas_call(
         body_kernel,
-        out_shape=jax.ShapeDtypeStruct((count, half, LANE), f32),
+        out_shape=outs,
         in_specs=[pl.BlockSpec(memory_space=pltpu.SMEM)] * 4
         + [pl.BlockSpec(memory_space=pltpu.HBM)] * (3 + len(tables)),
-        out_specs=pl.BlockSpec(memory_space=pltpu.VMEM),
+        out_specs=[pl.BlockSpec(memory_space=pltpu.VMEM)] * len(outs),
         scratch_shapes=scratch,
         compiler_params=pltpu.CompilerParams(
             vmem_limit_bytes=20 << 20, collective_id=0, has_side_effects=True
@@ -462,6 +518,19 @@
             )
         ],
     )
+    out = pl.pallas_call(
+        finish_kernel,
+        out_shape=shape((count, half, LANE), f32),
+        in_specs=[pl.BlockSpec(memory_space=pltpu.VMEM)] * len(parts),
+        out_specs=pl.BlockSpec(memory_space=pltpu.HBM),
+        scratch_shapes=[
+            pltpu.VMEM((3 * LANE, CHUNK * LANE), bf16),
+            pltpu.VMEM((CHUNK, half, LANE), f32),
+            dma((count // CHUNK,)),
+        ],
+        compiler_params=pltpu.CompilerParams(vmem_limit_bytes=16 << 20),
+        name="finish_rows",
+    )(*parts)
     return out.reshape(count, 1, 2 * pixels)
 
 

time: 39.5 us -> 36.4 us (0.922)
  Pallas kernels: 35.5 us -> 33.7 us
  local copies, waits for them, and re-layouts: 1.32 us -> 0 us
    pallas_call x1 -> x2, Pallas kernels: 35.5 us -> 33.7 us  [the longest x1 32 us: local(): pl.pallas_call(body_kernel, out_shape=outs, in_specs=[pl.BlockSpec(memory...]
    unnamed x1 -> x0, local copies, waits for them, and re-layouts: 1.32 us -> none
where the time goes in v3:
time: 36.4 us; the launch traced here: 36.3 us
  Pallas kernels  33.7 us (93%)
  between operations  2.59 us (7%)
    pallas_call x1, Pallas kernels, local(): pl.pallas_call(body_kernel, out_shape=outs, in_specs=[pl.BlockSpec(memory...  32 us
    pallas_call x1, Pallas kernels, local(): pl.pallas_call(finish_kernel, out_shape=shape((count, half, LANE), f32),...  1.66 us

profile of v3, /device:TPU:0, one launch (start us, length us, event | category | flops | bytes accessed | tf_op | source)
XLA Modules:
  0.0 36.3 jit_solution(6428045672074501077)
XLA Ops:
  2.6 32.0 %filter_rows.1 = (f32[56,64,128]{2,1,0:T(8,128)S(1)}, bf16[512,768]{1,0:T(8,128)(2,1)S(1)}, f32[8,64,128]{2,1,0:T(8,128)S(1)}, bf16[768,256]{1,0:T(8,128)(2,1)S(...) custom-call(s32[1]{0:T(128)S(6)} %copy.18.refs_0_, s32[1]{0:T(128)S(6)} %copy.19.refs_1_, s32[1]{0:T(128)S(6)} %copy.20.refs_2_, ...), custom_call_target="tpu_custom_call" | custom-call | tf_op jit(solution)/shard_map/filter_rows/pallas_call | solution.py:495
  34.6 1.7 %finish_rows.1 = f32[64,64,128]{2,1,0:T(8,128)} custom-call(f32[56,64,128]{2,1,0:T(8,128)S(1)} %get-tuple-element.11.out_ref, bf16[512,768]{1,0:T(8,128)(2,1)S(1)} %get-tuple-element.12.zk_ref, f32[8,64,128]{2,1,0:T(8,128)S(1)} %get-tuple-element.13.bias_ref, bf16[768,256]{1,0:T(8,128)(2,1)S(1)} %get-tuple-element.14.bwd_ref, ...), custom_call_target="tpu_custom_call" | custom-call | tf_op jit(solution)/shard_map/finish_rows/pallas_call | solution.py:521

commit v4 on v3

--- a/solution.py
+++ b/solution.py
@@ -19,9 +19,8 @@
 STACK = 80
 SUM_STEP = 1
 MODE_STEP = 3
-CORR_STEP = 6
+CORR_STEP = 5
 FIRST = 3
-AHEAD = 4
 MESH = pl.DeviceIdType.MESH
 
 
@@ -136,11 +135,11 @@
 NAMES = SCRATCH_NAMES + ("twiddle", "backward", "final")
 
 
-def inverse(zk_s, bwd_s, fin_s, tw_s, uk_s):
+def inverse(zk_s, bwd_s, fin_s, tw_s, uk_s, size=CHUNK):
     half = LANE // 2
-    u = dot(zk_s[...], bwd_s[...])
+    u = dot(zk_s[: size * half, :], bwd_s[...])
     cos, sin = tw_s[:half, :], tw_s[half:, :]
-    for i in range(CHUNK):
+    for i in range(size):
         re = u[i * half : (i + 1) * half, :LANE]
         im = u[i * half : (i + 1) * half, LANE:]
         high, low = split(jnp.concatenate([re * cos - im * sin, im * cos + re * sin], axis=0))
@@ -148,7 +147,7 @@
         uk_s[:LANE, cols] = high
         uk_s[LANE : 2 * LANE, cols] = low
         uk_s[2 * LANE :, cols] = high
-    return dot(fin_s[...], uk_s[...])
+    return dot(fin_s[...], uk_s[:, : size * LANE])
 
 
 def finish_kernel(out_ref, zk_ref, bias_ref, bwd_ref, fin_ref, tw_ref, y_ref, uk_s, res_s, sems):
@@ -178,7 +177,7 @@
     out_ref, zk_o, bias_o, bwd_s, fin_s, tw_s = refs[7 + len(NAMES) : 13 + len(NAMES)]
     rest = refs[13 + len(NAMES) :]
     (xs, got_s, gown_s, rs_s, sum_s, gx_s, bg_s, corr_s, edge_t, first_d,
-     main_s, back_s, shift_s, xk_s, yk_s, zk_s, uk_s, res_s, edge_s,
+     main_s, back_s, shift_s, xk_s, yk_s, zk_s, uk_s, edge_s,
      tsem, xsem, fsem, dsem, ex_send, ex_recv, rs_send, rs_recv, gx_send, gx_recv, ag_send, ag_recv,
      flat_s, dark_s) = rest[len(SCRATCH_NAMES) :]
     phi_s, first_s, sums_s, gain_s, fwd_s, coef_s = rest[: len(SCRATCH_NAMES)]
@@ -212,6 +211,7 @@
     load_d = pltpu.make_async_copy(dark_ref, dark_s, dsem)
     load_d.start()
     loads = [pltpu.make_async_copy(tables[i], held[i], tsem.at[i]) for i in range(len(NAMES))]
+    loads[0].start()
     corr_ref, blend_ref, pad_ref, cutoff_ref = scalar_refs
     pl.semaphore_wait(barrier, halves)
 
@@ -229,7 +229,7 @@
 
     for c in range(FIRST):
         exchange(c).start()
-    for load in loads:
+    for load in loads[1:]:
         load.start()
 
     block = GROUP * blocks
@@ -267,8 +267,7 @@
     load_f.wait()
     load_d.wait()
     load_x.wait()
-    for load in loads:
-        load.wait()
+    loads[0].wait()
 
     phi = phi_s[pl.ds(yy * MODES, MODES), :]
     for n1 in range(blocks):
@@ -280,6 +279,8 @@
     for k in range(1, halves):
         scatter(k).start()
 
+    for load in loads[1:]:
+        load.wait()
     corr = corr_ref[0]
     pad = pad_ref[0]
     blend = blend_ref[0].astype(jnp.float32)
@@ -301,25 +302,20 @@
     ).astype(jnp.float32)
 
     def receive(c):
-        exchange(c).wait()
-
-        @pl.when(False if isinstance(c, int) else jnp.logical_and(c >= SUM_STEP, c + AHEAD < chunks))
-        def _():
-            exchange(c + AHEAD).start()
-
         dark = dark_s[...]
         base = jnp.log(flat_s[...] - dark)
         own = xs[pl.ds(upper * count * blocks + c * span, span), :].reshape(CHUNK, blocks, LANE)
         own = base - jnp.log(own - dark)
+        exchange(c).wait()
         got = base - jnp.log(got_s[pl.ds(c * span, span), :].reshape(CHUNK, blocks, LANE) - dark)
         main_s[...] = jnp.where(upper == 1, got, own)
         back_s[...] = jnp.where(upper == 1, own, got)
 
-    def front(which, zk_s):
+    def front(which, zk_s, size=CHUNK):
         weight = jnp.clip((pixel + 0.5 - corr.astype(jnp.float32) * 0.5) / blend + 0.5, 0.0, 1.0)
         lanes = lax.broadcasted_iota(jnp.int32, (blocks, LANE), 1)
         lanes48 = lax.broadcasted_iota(jnp.int32, (STACK - blocks, LANE), 1)
-        for i in range(CHUNK):
+        for i in range(size):
             main = main_s[i]
             back = back_s[i]
             edge_s[0, i : i + 1, :] = jnp.broadcast_to(main[blocks - 1 : blocks, LANE - 1 :], (1, LANE))
@@ -334,9 +330,9 @@
             xk_s[:STACK, cols] = high
             xk_s[STACK : 2 * STACK, cols] = low
             xk_s[2 * STACK :, cols] = high
-        y = dot(first_d[...], xk_s[...])
+        y = dot(first_d[...], xk_s[:, : size * LANE])
         cos, sin = tw_s[:half, :], tw_s[half:, :]
-        for i in range(CHUNK):
+        for i in range(size):
             re = y[:half, i * LANE : (i + 1) * LANE]
             im = y[half:, i * LANE : (i + 1) * LANE]
             high, low = split(jnp.concatenate([re * cos + im * sin, im * cos - re * sin], axis=1))
@@ -344,10 +340,10 @@
             yk_s[rows, :wide] = high
             yk_s[rows, wide : 2 * wide] = low
             yk_s[rows, 2 * wide :] = high
-        gain = gain_s[pl.ds(which * half, half), :]
+        gain = gain_s[which * half : (which + 1) * half, :]
         gain2 = jnp.concatenate([gain, gain], axis=1)
-        z = dot(yk_s[...], fwd_s[...])
-        for i in range(CHUNK):
+        z = dot(yk_s[: size * half, :], fwd_s[...])
+        for i in range(size):
             rows = slice(i * half, (i + 1) * half)
             high, low = split(z[rows] * gain2)
             zk_s[rows, :wide] = high
@@ -355,80 +351,78 @@
             zk_s[rows, 2 * wide :] = high
 
     def edges(which, i):
-        tail = edge_t[pl.ds(which * LANE, half), :]
-        ahead = edge_t[pl.ds(which * LANE + half, half), :]
+        tail = edge_t[which * LANE : which * LANE + half, :]
+        ahead = edge_t[which * LANE + half : (which + 1) * LANE, :]
         return edge_s[0, i : i + 1, :] * tail + edge_s[1, i : i + 1, :] * ahead
 
-    def step(v, carry):
-        is_mode = v == MODE_STEP
-        c = v - (v > MODE_STEP).astype(jnp.int32)
-
-        @pl.when(v == SUM_STEP)
-        def _():
-            for k in range(1, halves):
-                scatter(k).wait()
-            sum_s[...] = gown_s[pl.ds(yy * block, block), :] + rs_s[1] + rs_s[2] + rs_s[3]
-            across().start()
-            for c in range(FIRST, AHEAD + SUM_STEP):
-                exchange(c).start()
-
-        @pl.when(is_mode)
-        def _():
-            across().wait()
-            mine = sum_s[...].reshape(GROUP, blocks, LANE)
-            theirs = gx_s[...].reshape(GROUP, blocks, LANE)
-            main_s[:GROUP] = jnp.where(upper == 1, theirs, mine)
-            back_s[:GROUP] = jnp.where(upper == 1, mine, theirs)
-
-        @pl.when(v == CORR_STEP)
-        def _():
-            for k in range(1, halves):
-                gather(k).wait()
-            coef = coef_s[pl.ds(place * count, count), :]
-            for n1 in range(0, half, 2):
-                pair = [bg_s[pl.ds(n1 + j, MODES, stride=half), :] for j in range(2)]
-                high, low = split(jnp.concatenate(pair, axis=1))
-                fix = dot(coef, jnp.concatenate([high, low, high], axis=0))
-                for j in range(2):
-                    corr_s[pl.ds(n1 + j, count, stride=half), :] = fix[:, j * LANE : (j + 1) * LANE]
-
-            def mend(i, carry):
-                out_ref[i] = out_ref[i] + corr_s[pl.ds(i * half, half), :]
-                return carry
-
-            lax.fori_loop(0, (CORR_STEP - 1) * CHUNK, mend, 0)
-
-        @pl.when(jnp.logical_not(is_mode))
-        def _():
-            receive(c)
-
-        which = is_mode.astype(jnp.int32)
-        front(which, zk_s)
+    def mode_sums():
+        for k in range(1, halves):
+            scatter(k).wait()
+        sum_s[...] = gown_s[pl.ds(yy * block, block), :] + rs_s[1] + rs_s[2] + rs_s[3]
+        across().start()
+        for c in range(FIRST, chunks):
+            exchange(c).start()
+
+    def data_step(c, corrected):
+        receive(c)
+        front(0, zk_s)
         o = inverse(zk_s, bwd_s, fin_s, tw_s, uk_s)
         for i in range(CHUNK):
-            res_s[i] = o[:, i * LANE : (i + 1) * LANE] + edges(which, i)
-
-        @pl.when(is_mode)
+            line = o[:, i * LANE : (i + 1) * LANE] + edges(0, i)
+            if corrected:
+                line = line + corr_s[pl.ds((c * CHUNK + i) * half, half), :]
+            out_ref[c * CHUNK + i] = line
+
+    def early(c, carry):
+        @pl.when(c == SUM_STEP)
         def _():
-            for i in range(GROUP):
-                order = jnp.bitwise_and(yy * GROUP + i, KMAX - 1)
-                keep = jnp.where(order < cutoff_ref[0], 1.0, 0.0)
-                bg_s[i * half : (i + 1) * half, :] = res_s[i] * keep
-            for k in range(1, halves):
-                gather(k).start()
-
-        @pl.when(jnp.logical_and(jnp.logical_not(is_mode), v < CORR_STEP))
-        def _():
-            out_ref[pl.ds(c * CHUNK, CHUNK)] = res_s[...]
-
-        @pl.when(v >= CORR_STEP)
-        def _():
-            rows = corr_s[pl.ds(c * CHUNK * half, CHUNK * half), :]
-            out_ref[pl.ds(c * CHUNK, CHUNK)] = res_s[...] + rows.reshape(CHUNK, half, LANE)
-
+            mode_sums()
+
+        data_step(c, False)
         return carry
 
-    lax.fori_loop(0, chunks, step, 0)
+    def middle(c, carry):
+        data_step(c, False)
+        return carry
+
+    def late(c, carry):
+        data_step(c, True)
+        return carry
+
+    lax.fori_loop(0, MODE_STEP, early, 0)
+
+    across().wait()
+    mine = sum_s[...].reshape(GROUP, blocks, LANE)
+    theirs = gx_s[...].reshape(GROUP, blocks, LANE)
+    main_s[:GROUP] = jnp.where(upper == 1, theirs, mine)
+    back_s[:GROUP] = jnp.where(upper == 1, mine, theirs)
+    front(1, zk_s, GROUP)
+    o = inverse(zk_s, bwd_s, fin_s, tw_s, uk_s, GROUP)
+    for i in range(GROUP):
+        order = jnp.bitwise_and(yy * GROUP + i, KMAX - 1)
+        keep = jnp.where(order < cutoff_ref[0], 1.0, 0.0)
+        bg_s[i * half : (i + 1) * half, :] = (o[:, i * LANE : (i + 1) * LANE] + edges(1, i)) * keep
+    for k in range(1, halves):
+        gather(k).start()
+
+    lax.fori_loop(MODE_STEP, CORR_STEP, middle, 0)
+
+    for k in range(1, halves):
+        gather(k).wait()
+    coef = coef_s[pl.ds(place * count, count), :]
+    for n1 in range(0, half, 2):
+        pair = [bg_s[pl.ds(n1 + j, MODES, stride=half), :] for j in range(2)]
+        high, low = split(jnp.concatenate(pair, axis=1))
+        fix = dot(coef, jnp.concatenate([high, low, high], axis=0))
+        for j in range(2):
+            corr_s[pl.ds(n1 + j, count, stride=half), :] = fix[:, j * LANE : (j + 1) * LANE]
+
+    def mend(i, carry):
+        out_ref[i] = out_ref[i] + corr_s[pl.ds(i * half, half), :]
+        return carry
+
+    lax.fori_loop(0, CORR_STEP * CHUNK, mend, 0)
+    lax.fori_loop(CORR_STEP, chunks - 1, late, 0)
     for i in range(CHUNK):
         bias_o[i] = corr_s[((chunks - 1) * CHUNK + i) * half : ((chunks - 1) * CHUNK + i + 1) * half, :]
     receive(chunks - 1)
@@ -469,7 +463,6 @@
         pltpu.VMEM((CHUNK * half, 6 * LANE), bf16),
         pltpu.VMEM((CHUNK * half, 6 * LANE), bf16),
         pltpu.VMEM((3 * LANE, CHUNK * LANE), bf16),
-        pltpu.VMEM((CHUNK, half, LANE), f32),
         pltpu.VMEM((2, CHUNK, LANE), f32),
         dma((len(tables),)),
         dma,

time: 36.4 us -> 36.4 us (level)
  no operation moved by 1% of the time
where the time goes in v4:
time: 36.4 us; the launch traced here: 36.3 us
  Pallas kernels  33.7 us (93%)
  between operations  2.59 us (7%)
    pallas_call x1, Pallas kernels, local(): pl.pallas_call(body_kernel, out_shape=outs, in_specs=[pl.BlockSpec(memory...  32 us
    pallas_call x1, Pallas kernels, local(): pl.pallas_call(finish_kernel, out_shape=shape((count, half, LANE), f32),...  1.66 us

profile of v4, /device:TPU:0, one launch (start us, length us, event | category | flops | bytes accessed | tf_op | source)
XLA Modules:
  0.0 36.3 jit_solution(5082487515964170874)
XLA Ops:
  2.6 32.0 %filter_rows.1 = (f32[56,64,128]{2,1,0:T(8,128)S(1)}, bf16[512,768]{1,0:T(8,128)(2,1)S(1)}, f32[8,64,128]{2,1,0:T(8,128)S(1)}, bf16[768,256]{1,0:T(8,128)(2,1)S(...) custom-call(s32[1]{0:T(128)S(6)} %copy.18.refs_0_, s32[1]{0:T(128)S(6)} %copy.19.refs_1_, s32[1]{0:T(128)S(6)} %copy.20.refs_2_, ...), custom_call_target="tpu_custom_call" | custom-call | tf_op jit(solution)/shard_map/filter_rows/pallas_call | solution.py:488
  34.6 1.7 %finish_rows.1 = f32[64,64,128]{2,1,0:T(8,128)} custom-call(f32[56,64,128]{2,1,0:T(8,128)S(1)} %get-tuple-element.11.out_ref, bf16[512,768]{1,0:T(8,128)(2,1)S(1)} %get-tuple-element.12.zk_ref, f32[8,64,128]{2,1,0:T(8,128)S(1)} %get-tuple-element.13.bias_ref, bf16[768,256]{1,0:T(8,128)(2,1)S(1)} %get-tuple-element.14.bwd_ref, ...), custom_call_target="tpu_custom_call" | custom-call | tf_op jit(solution)/shard_map/finish_rows/pallas_call | solution.py:514
